TPU v7x, 128 devices: a whole 4x4x4 slice. The times are simulated.
128 devices in a mesh: row: 16 (over x, z_lo, core), col: 8 (over z_hi, y).
Axes of the slice: x: 4, y: 4, z: 4 (z_hi: 2, z_lo: 2; z = z_hi * 2 + z_lo), core: 2. Of those that a mesh axis runs over, the one named last changes fastest.
Arguments:
- out_grad: bfloat16 [512, 16384], P('col', 'row'), may hold values from -6 to 6
- gate_saved: bfloat16 [512, 26624], P('row', 'col'), may hold values from -8 to 8
- up_saved: bfloat16 [512, 26624], P('row', 'col'), may hold values from -6 to 6
- gate_weight: bfloat16 [16384, 26624], P('row', 'col'), may hold values from -0.046875 to 0.046875
- up_weight: bfloat16 [16384, 26624], P('row', 'col'), may hold values from -0.046875 to 0.046875
- down_weight: bfloat16 [26624, 16384], P('col', 'row'), may hold values from -0.0390625 to 0.0390625
Outputs:
- input_grad: bfloat16 [512, 16384], P('col', 'row')
All inputs are finite; a program needn't handle non-finite values.
Results may differ from a plain program's by a relative error of at most 0.0049.
Values may be sent and summed in bfloat16 or wider, within the bound.
A program may use at most 128 MiB of HBM per device.

v0:
```python
import jax
import jax.numpy as jnp
from jax import lax
from jax.sharding import PartitionSpec as P


def joined_along(blocks, dim):
    shape = list(blocks.shape[1:])
    shape[dim] *= blocks.shape[0]
    return jnp.moveaxis(blocks, 0, dim).reshape(shape)


def sent_to_all(shard, axis):
    copies = jnp.broadcast_to(shard, (lax.axis_size(axis), *shard.shape))
    return lax.all_to_all(copies, axis, split_axis=0, concat_axis=0, tiled=True)


def gather_directly(shard, axis, dim):
    return joined_along(sent_to_all(shard, axis), dim)


def in_blocks(shard, dim, count):
    before, after = (shard.shape[:dim], shard.shape[dim + 1 :])
    return jnp.moveaxis(shard.reshape(*before, count, -1, *after), dim, 0)


def sent_and_summed(shard, axis, dim):
    blocks = in_blocks(shard, dim, lax.axis_size(axis))
    arrived = lax.all_to_all(blocks, axis, split_axis=0, concat_axis=0, tiled=True)
    return arrived.sum(axis=0)


def contract_last(left, right):
    return lax.dot_general(
        left, right, (((1,), (1,)), ((), ())), preferred_element_type=jnp.float32
    )


def swiglu_back(hidden_grad, gate_saved, up_saved):
    gate_float = gate_saved.astype(jnp.float32)
    up_float = up_saved.astype(jnp.float32)
    sigmoid_gate = jax.nn.sigmoid(gate_float)
    up_grad = (hidden_grad * gate_float * sigmoid_gate).astype(jnp.bfloat16)
    gate_grad = (
        hidden_grad * up_float * sigmoid_gate * (1.0 + gate_float * (1.0 - sigmoid_gate))
    ).astype(jnp.bfloat16)
    return (gate_grad, up_grad)


def per_device(out_grad, gate_saved, up_saved, gate_weight, up_weight, down_weight):
    partial_hidden = contract_last(gather_directly(out_grad, "col", 0), down_weight)
    hidden_grad = lax.psum_scatter(partial_hidden, "row", scatter_dimension=0, tiled=True)
    gate_grad, up_grad = swiglu_back(hidden_grad, gate_saved, up_saved)
    block_pair = lax.all_gather((gate_grad, up_grad), "row", axis=0, tiled=True)
    partial_input = contract_last(block_pair[0], gate_weight) + contract_last(
        block_pair[1], up_weight
    )
    return sent_and_summed(partial_input, "col", 0).astype(jnp.bfloat16)


def solution(mesh):
    placed = (
        P("col", "row"),
        P("row", "col"),
        P("row", "col"),
        P("row", "col"),
        P("row", "col"),
        P("col", "row"),
    )
    return jax.shard_map(
        per_device, mesh=mesh, in_specs=placed, out_specs=P("col", "row"), check_vma=False
    )
```

profile of v0, /device:TPU:0, one launch (start us, length us, event | category | flops | bytes accessed | tf_op | source)
XLA Modules:
  0.0 246.3 jit_solution(9135726643115519771)
XLA Ops:
  6.5 0.0 reduce-scatter.2.cloned.1.call-start
  6.5 1.0 broadcast_in_dim.3
  7.6 24.9 %all_to_all.10 = bf16[8,64,1024]{2,1,0:T(8,128)(2,1)S(1)} all-to-all(bf16[8,64,1024]{2,1,0:T(8,128)(2,1)S(1)} %broadcast_in_dim.3), channel_id=1, replica_groups=mesh['row'=16,'col'=8] {'col'}, dimensions={0} | all-to-all | bytes 2097152 | tf_op jit(solution)/shard_map/all_to_all | solution.py:15
  32.5 8.7 %fusion.8 = f32[512,3328]{1,0:T(8,128)} fusion(bf16[512,1024]{1,0:T(8,128)(2,1)S(1)} %bitcast.9, bf16[3328,1024]{1,0:T(8,128)(2,1)} %param.11), kind=kOutput, calls=%fused_computation.12 | convolution fusion | flops 3489660928 | bytes 14680064 | tf_op jit(solution)/shard_map/dot_general | solution.py:34
  41.1 0.0 copy-start
  41.1 0.0 copy-start.1
  41.1 0.0 reduce-scatter.2.cloned.1.call-update
  41.1 0.0 all-gather.3.cloned.1.call-start
  41.2 79.0 %reduce-scatter.2.cloned.1.call-done = f32[32,3328]{1,0:T(8,128)} async-done(((f32[512,3328]{1,0:T(8,128)}), f32[32,3328]{1,0:T(8,128)}) %reduce-scatter.2.cloned.1.call-update) | async-done | bytes 426000 | tf_op jit(solution)/shard_map/reduce_scatter | solution.py:52
  120.2 0.0 copy-done
  120.2 0.0 copy-done.1
  120.2 2.0 fusion.7
  122.2 0.0 all-gather.3.cloned.1.call-update
  122.2 0.0 all-gather.5.cloned.1.call-start
  122.3 0.7 all-gather.5.cloned.1.call-update
  123.0 36.1 %all-gather.3.cloned.1.call-done = bf16[512,3328]{1,0:T(8,128)(2,1)} async-done(((bf16[32,3328]{1,0:T(8,128)(2,1)}), bf16[512,3328]{1,0:T(8,128)(2,1)}) %all-gather.3.cloned.1.call-update) | async-done | bytes 3407888 | tf_op jit(solution)/shard_map/all_gather | solution.py:54
  159.1 6.9 %fusion.9 = f32[512,1024]{1,0:T(8,128)S(1)} fusion(bf16[512,3328]{1,0:T(8,128)(2,1)} %all-gather.3.cloned.1.call-done, bf16[1024,3328]{1,0:T(8,128)(2,1)} %param.9), kind=kOutput, calls=%fused_computation.13 | convolution fusion | flops 3489660928 | bytes 12320768 | tf_op jit(solution)/shard_map/dot_general | solution.py:34
  166.0 30.8 %all-gather.5.cloned.1.call-done = bf16[512,3328]{1,0:T(8,128)(2,1)} async-done(((bf16[32,3328]{1,0:T(8,128)(2,1)}), bf16[512,3328]{1,0:T(8,128)(2,1)}) %all-gather.5.cloned.1.call-update) | async-done | bytes 3407888 | tf_op jit(solution)/shard_map/all_gather | solution.py:54
  196.8 6.9 %convolution_add_fusion = f32[512,1024]{1,0:T(8,128)S(1)} fusion(f32[512,1024]{1,0:T(8,128)S(1)} %fusion.9, bf16[512,3328]{1,0:T(8,128)(2,1)} %all-gather.5.cloned.1.call-done, bf16[1024,3328]{1,0:T(8,128)(2,1)} %param.10), kind=kOutput, calls=%fused_computation | convolution fusion | flops 3490185216 | bytes 14417920 | tf_op jit(solution)/shard_map/dot_general | solution.py:34
  203.8 35.2 %all_to_all.11 = f32[8,64,1024]{2,1,0:T(8,128)S(1)} all-to-all(f32[8,64,1024]{2,1,0:T(8,128)S(1)} %bitcast.8), channel_id=1, replica_groups=mesh['row'=16,'col'=8] {'col'}, dimensions={0} | all-to-all | bytes 4194304 | tf_op jit(solution)/shard_map/all_to_all | solution.py:29
  238.9 0.8 reduce_sum.9
Async XLA Ops:
  6.5 113.7 %reduce-scatter.2.cloned.1.call-start = ((), (), s32[]{:S(2)}) async-start(), calls=%async_computation.3 | async-start | bytes 7241728 | tf_op jit(solution)/shard_map/reduce_scatter | solution.py:52
  41.1 79.1 %copy-start = (bf16[32,3328]{1,0:T(8,128)(2,1)S(1)}, bf16[32,3328]{1,0:T(8,128)(2,1)}, u32[]{:S(2)}) copy-start(bf16[32,3328]{1,0:T(8,128)(2,1)} %param.7) | copy-start | bytes 638980
  41.1 79.1 %copy-start.1 = (bf16[32,3328]{1,0:T(8,128)(2,1)S(1)}, bf16[32,3328]{1,0:T(8,128)(2,1)}, u32[]{:S(2)}) copy-start(bf16[32,3328]{1,0:T(8,128)(2,1)} %param.8) | copy-start | bytes 638980
  41.1 117.9 %all-gather.3.cloned.1.call-start = ((), (), s32[]{:S(2)}) async-start(), calls=%async_computation.4 | async-start | bytes 3620864 | tf_op jit(solution)/shard_map/all_gather | solution.py:54
  122.2 74.6 %all-gather.5.cloned.1.call-start = ((), (), s32[]{:S(2)}) async-start(), calls=%async_computation.5 | async-start | bytes 3620864 | tf_op jit(solution)/shard_map/all_gather | solution.py:54
Sparse Core Ops, SparseCore 0:
  41.3 78.9 reduce-scatter.1
  122.3 36.6 all-gather.2
  160.8 35.9 all-gather.4
where the time goes:
time: 247 us; the launch traced here: 246 us
  waiting for transfers between devices  147 us (60%)
  blocking collectives  60.1 us (24%)
  matrix products  22.5 us (9%)
  between operations  13.1 us (5%)
  other arithmetic  2.77 us (1%)
    reduce_scatter x1, waiting for transfers between devices, per_device(): lax.psum_scatter(partial_hidden, 'row', scatter_dimension=0, tiled=True)  79 us
    all_gather x2, waiting for transfers between devices, per_device(): block_pair = lax.all_gather((gate_grad, up_grad), 'row', axis=0, tiled=True)  66.9 us
    all_to_all x1, blocking collectives, sent_and_summed(): lax.all_to_all(blocks, axis, split_axis=0, concat_axis=0, tiled=True)  35.2 us
    all_to_all x1, blocking collectives, sent_to_all(): return lax.all_to_all(copies, axis, split_axis=0, concat_axis=0, tiled=True)  24.9 us
    dot_general x3, matrix products, contract_last(): lax.dot_general(left, right, (((1,), (1,)), ((), ())), preferred_element_...  22.5 us
  transfers between devices with their start and end apart: 3, of which 3 were waited for; matrix products, arithmetic and copies ran while one was open for 3% of the time, Pallas kernels for 0%

commit v1 on v0

v1 whole, which is shorter than its diff:
```python
import jax
import jax.numpy as jnp
from jax import lax
from jax.experimental import pallas as pl
from jax.experimental.pallas import tpu as pltpu
from jax.sharding import PartitionSpec as P

MESH = pl.DeviceIdType.MESH
F32, BF16 = jnp.float32, jnp.bfloat16

CHUNKS = 2
LANES = 256


def contract_last(left, right):
    return lax.dot_general(
        left, right, (((1,), (1,)), ((), ())), preferred_element_type=F32
    )


class Copies:
    def __init__(self, send_sems, recv_sems):
        self.send_sems, self.recv_sems, self.made = send_sems, recv_sems, {}

    def send(self, name, src, dst, device):
        index = len(self.made)
        copy = pltpu.make_async_remote_copy(
            src_ref=src,
            dst_ref=dst,
            send_sem=self.send_sems.at[index],
            recv_sem=self.recv_sems.at[index],
            device_id=device,
            device_id_type=MESH,
        )
        copy.start()
        self.made[name] = copy

    def arrived(self, *names):
        for name in names:
            self.made[name].wait_recv()

    def finish(self):
        for copy in self.made.values():
            copy.wait_send()


def kernel(
    og, gs, us, gw, uw, dw, out,
    tokens, wd, wg, wu, gv, uv,
    own1, own2, give1, give2, got1, got2,
    xs1, xr1, xs2, xr2, zs1, zr1, keep1, zs2, zr2,
    grads1, grads2, total, ys, yr, keep3, hs, hr,
    local_sems, send_sems, recv_sems,
):
    rows = gs.shape[0] // CHUNKS
    wide1, wide2 = own1.shape[-1], own2.shape[-1]
    half1, half2, half3 = wide1 // 2, wide2 // 2, out.shape[-1] // 2
    row, col = lax.axis_index("row"), lax.axis_index("col")
    x, zl, c = row // 4, (row // 2) % 2, row % 2
    zh, y = col // 4, col % 4

    def at_row(x_, zl_, c_):
        return {"row": (x_ % 4) * 4 + zl_ * 2 + c_}

    def at_col(zh_, y_):
        return {"col": zh_ * 4 + y_ % 4}

    core, zn = at_row(x, zl, 1 - c), at_row(x, 1 - zl, c)
    xp, xm = at_row(x + 1, zl, c), at_row(x + 3, zl, c)
    zp, yp, ym = at_col(1 - zh, y), at_col(zh, y + 1), at_col(zh, y + 3)

    def place(zh_, y_):
        y_ = y_ % 4
        return ((zh_ * 2 + y_ // 2 - x + 4) % 4) * 2 + (y_ % 2 + zl) % 2

    loads = {}

    def load(name, src, dst):
        copy = pltpu.make_async_copy(src, dst, local_sems.at[len(loads)])
        copy.start()
        loads[name] = copy

    mine = place(zh, y)
    for t in range(CHUNKS):
        for c_ in range(2):
            load(
                f"t{t}{c_}",
                og.at[pl.ds(c_ * 32 + t * rows, rows)],
                tokens.at[t, (c_ + c) % 2, mine],
            )
    load("d2", dw.at[pl.ds(wide1, wide2)], wd.at[pl.ds(wide1, wide2)])
    load("d1", dw.at[pl.ds(0, wide1)], wd.at[pl.ds(0, wide1)])
    load("gv", gs, gv)
    load("uv", us, uv)
    load("wg", gw, wg)
    load("wu", uw, wu)

    barrier = pltpu.get_barrier_semaphore()
    peers = (core, zn, xp, xm, zp, yp, ym)
    for peer in peers:
        pl.semaphore_signal(barrier, inc=1, device_id=peer, device_id_type=MESH)
    pl.semaphore_wait(barrier, len(peers))

    net = Copies(send_sems, recv_sems)

    def spread(t, z_, name):
        here = tokens.at[t, :, place(z_, y)]
        net.send(f"a{name}+{t}", here, here, yp)
        net.send(f"a{name}-{t}", here, here, ym)

    def pass_on(t, z_, name):
        net.arrived(f"a{name}+{t}", f"a{name}-{t}")
        left, right = tokens.at[t, 0, place(z_, y + 3)], tokens.at[t, 1, place(z_, y + 1)]
        net.send(f"f{name}+{t}", left, left, yp)
        net.send(f"f{name}-{t}", right, right, ym)

    def gather_1(t):
        loads[f"t{t}0"].wait()
        loads[f"t{t}1"].wait()
        here = tokens.at[t, :, mine]
        net.send(f"az{t}", here, here, zp)
        spread(t, zh, "o")

    def gather_2(t):
        net.arrived(f"az{t}")
        spread(t, 1 - zh, "p")

    def gather_3(t):
        pass_on(t, zh, "o")

    def gather_4(t):
        pass_on(t, 1 - zh, "p")

    def gather_5(t):
        net.arrived(f"fo+{t}", f"fo-{t}", f"fp+{t}", f"fp-{t}")

    def first_dot(t, own, give, got, offset, name):
        wide = own.shape[-1]

        def tile(n, carry):
            left = tokens[t].reshape(16 * rows, -1)
            here = pl.ds(pl.multiple_of(offset + n * LANES, LANES), LANES)
            there = pl.ds(pl.multiple_of(n * LANES, LANES), LANES)
            share = contract_last(left, wd[here, :]).reshape(2, 8, rows, LANES)
            own[t, :, :, there] = share[0]
            give[t, :, :, there] = share[1].astype(BF16)
            return carry

        lax.fori_loop(0, wide // LANES, tile, 0)
        net.send(f"{name}c{t}", give.at[t], got.at[t], core)

    def dot_1(t):
        first_dot(t, own1, give1, got1, 0, "b1")

    def dot_2(t):
        first_dot(t, own2, give2, got2, wide1, "b2")

    def x_out(name, t, xs, xr, part, half):
        for way, m, k, lo, to in (
            (0, 0, 2, 0, xp), (1, 0, 2, half, xm), (0, 1, 1, half, xp), (1, 1, 3, 0, xm),
        ):
            xs[t, way, m] = part(k, lo).astype(BF16)
            net.send(f"{name}{way}{m}{t}", xs.at[t, way, m], xr.at[t, way, m], to)

    def x_on(name, t, xs, xr, part, half):
        for way, k, lo, to in ((0, 1, 0, xp), (1, 3, half, xm)):
            net.arrived(f"{name}{way}0{t}")
            xs[t, way, 2] = (part(k, lo) + xr[t, way, 0].astype(F32)).astype(BF16)
            net.send(f"{name}{way}2{t}", xs.at[t, way, 2], xr.at[t, way, 2], to)

    def x_in(name, t, xr, part, half, finish):
        net.arrived(*(f"{name}{way}{m}{t}" for way in (0, 1) for m in (1, 2)))
        for lo, m in ((0, 2), (half, 1)):
            finish(
                lo,
                part(0, lo)
                + xr[t, 0, m].astype(F32)
                + xr[t, 1, 3 - m].astype(F32),
            )

    def part1(t):
        def part(k, lo):
            here = (t, pl.ds(2 * k, 2), slice(None), pl.ds(lo, half1))
            return own1[here] + got1[here].astype(F32)

        return part

    def part2(t):
        def part(k, lo):
            here = (t, 2 * k, slice(None), pl.ds(lo, half2))
            arrived = zr2[t, k, :, pl.ds(lo, half2)]
            return own2[here] + got2[here].astype(F32) + arrived.astype(F32)

        return part

    def sum1_1(t):
        net.arrived(f"b1c{t}")
        x_out("b1x", t, xs1, xr1, part1(t), half1)

    def sum1_2(t):
        x_on("b1x", t, xs1, xr1, part1(t), half1)

    def sum1_3(t):
        def finish(lo, value):
            zs1[t, :, pl.ds(lo, half1)] = value[1].astype(BF16)
            keep1[t, :, pl.ds(lo, half1)] = value[0]

        x_in("b1x", t, xr1, part1(t), half1, finish)
        net.send(f"b1z{t}", zs1.at[t], zr1.at[t], zn)

    def sum2_1(t):
        net.arrived(f"b2c{t}")
        for k in range(4):
            zs2[t, k] = (own2[t, 2 * k + 1] + got2[t, 2 * k + 1].astype(F32)).astype(BF16)
        net.send(f"b2z{t}", zs2.at[t], zr2.at[t], zn)

    def sum2_2(t):
        net.arrived(f"b2z{t}")
        x_out("b2x", t, xs2, xr2, part2(t), half2)

    def sum2_3(t):
        x_on("b2x", t, xs2, xr2, part2(t), half2)

    def swiglu_back(t, hidden, grads, lo, offset):
        width = hidden.shape[-1]
        here = (pl.ds(t * rows, rows), pl.ds(offset + lo, width))
        gate, up = gv[here].astype(F32), uv[here].astype(F32)
        s = jax.nn.sigmoid(gate)
        there = pl.ds(lo, width)
        grads[t, 1, 0, 0, :, there] = (hidden * gate * s).astype(BF16)
        grads[t, 0, 0, 0, :, there] = (
            hidden * up * s * (1.0 + gate * (1.0 - s))
        ).astype(BF16)

    def sum1_4(t):
        net.arrived(f"b1z{t}")
        for lo in range(0, wide1, LANES):
            there = pl.ds(lo, LANES)
            hidden = keep1[t, :, there] + zr1[t, :, there].astype(F32)
            swiglu_back(t, hidden, grads1, lo, 0)

    def sum2_4(t):
        def finish(lo, value):
            swiglu_back(t, value, grads2, lo, wide1)

        x_in("b2x", t, xr2, part2(t), half2, finish)

    def block(grads, t, core_, e, lo=None, width=None):
        if lo is None:
            return grads.at[t, :, core_, e]
        return grads.at[t, :, core_, e, :, pl.ds(lo, width)]

    def to_core(name, grads, t, e):
        net.send(f"{name}p{e}{t}", block(grads, t, 0, e), block(grads, t, 1, e), core)

    def to_x(name, grads, t, z_):
        net.send(f"{name}x{6 + z_}{t}", block(grads, t, 0, z_), block(grads, t, 0, 6 + z_), xp)
        net.send(f"{name}x{2 + z_}{t}", block(grads, t, 0, z_), block(grads, t, 0, 2 + z_), xm)

    def on_x(name, grads, t, z_, half):
        net.arrived(f"{name}x{6 + z_}{t}")
        net.send(
            f"{name}l{z_}{t}",
            block(grads, t, 0, 6 + z_, 0, half),
            block(grads, t, 0, 4 + z_, 0, half),
            xp,
        )
        net.arrived(f"{name}x{2 + z_}{t}")
        net.send(
            f"{name}r{z_}{t}",
            block(grads, t, 0, 2 + z_, half, half),
            block(grads, t, 0, 4 + z_, half, half),
            xm,
        )

    def to_z(name, grads, t, e):
        net.send(f"{name}z{e}{t}", block(grads, t, 0, e), block(grads, t, 0, e + 1), zn)

    def all1_1(t):
        to_z("c1", grads1, t, 0)
        to_x("c1", grads1, t, 0)
        to_core("c1", grads1, t, 0)

    def all1_2(t):
        net.arrived(f"c1z0{t}")
        to_x("c1", grads1, t, 1)
        to_core("c1", grads1, t, 1)

    def all1_3(t):
        for z_ in range(2):
            on_x("c1", grads1, t, z_, half1)
            to_core("c1", grads1, t, 6 + z_)
            to_core("c1", grads1, t, 2 + z_)

    def all1_4(t):
        for z_ in range(2):
            net.arrived(f"c1l{z_}{t}", f"c1r{z_}{t}")
            to_core("c1", grads1, t, 4 + z_)

    def all1_5(t):
        net.arrived(*(f"c1p{e}{t}" for e in range(8)))

    def all2_1(t):
        to_x("c2", grads2, t, 0)
        to_z("c2", grads2, t, 0)
        to_core("c2", grads2, t, 0)

    def all2_2(t):
        on_x("c2", grads2, t, 0, half2)
        for e in (6, 2):
            to_z("c2", grads2, t, e)
            to_core("c2", grads2, t, e)

    def all2_3(t):
        net.arrived(f"c2l0{t}", f"c2r0{t}")
        to_z("c2", grads2, t, 4)
        to_core("c2", grads2, t, 4)

    def all2_4(t):
        for e in (0, 6, 2, 4):
            net.arrived(f"c2z{e}{t}")
            to_core("c2", grads2, t, e + 1)

    def all2_5(t):
        net.arrived(*(f"c2p{e}{t}" for e in range(8)))

    def second_dot(t, grads, offset, first):
        def tile(n, carry):
            there = pl.ds(pl.multiple_of(n * LANES, LANES), LANES)
            here = (there, pl.ds(offset, grads.shape[-1]))
            wide = grads.shape[-1]
            share = contract_last(grads[t, 0].reshape(16 * rows, wide), wg[here])
            share += contract_last(grads[t, 1].reshape(16 * rows, wide), wu[here])
            share = share.reshape(2, 8, rows, LANES)
            total[t, :, :, :, there] = share if first else total[t, :, :, :, there] + share
            return carry

        lax.fori_loop(0, total.shape[-1] // LANES, tile, 0)

    def dot_3(t):
        second_dot(t, grads1, 0, True)

    def dot_4(t):
        second_dot(t, grads2, wide1, False)

    def part3(t, j, lo):
        return [
            total[t, :, place((zh + za) % 2, y + j), :, pl.ds(lo, half3)] for za in range(2)
        ]

    def down_1(t):
        for way, m, j, lo, to in (
            (0, 0, 2, 0, yp), (1, 0, 2, half3, ym), (0, 1, 1, half3, yp), (1, 1, 3, 0, ym),
        ):
            for za, value in enumerate(part3(t, j, lo)):
                ys[t, way, m, za] = value.astype(BF16)
            net.send(f"d{way}{m}{t}", ys.at[t, way, m], yr.at[t, way, m], to)

    def down_2(t):
        for way, j, lo, to in ((0, 1, 0, yp), (1, 3, half3, ym)):
            net.arrived(f"d{way}0{t}")
            for za, value in enumerate(part3(t, j, lo)):
                ys[t, way, 2, za] = (value + yr[t, way, 0, za].astype(F32)).astype(BF16)
            net.send(f"d{way}2{t}", ys.at[t, way, 2], yr.at[t, way, 2], to)

    def down_3(t):
        net.arrived(*(f"d{way}{m}{t}" for way in (0, 1) for m in (1, 2)))
        for lo, m in ((0, 2), (half3, 1)):
            for za, value in enumerate(part3(t, 0, lo)):
                value = (
                    value
                    + yr[t, 0, m, za].astype(F32)
                    + yr[t, 1, 3 - m, za].astype(F32)
                )
                if za:
                    hs[t, :, :, pl.ds(lo, half3)] = value.astype(BF16)
                else:
                    keep3[t, :, :, pl.ds(lo, half3)] = value
        net.send(f"dz{t}", hs.at[t], hr.at[t], zp)

    def down_4(t):
        net.arrived(f"dz{t}")
        value = (keep3[t] + hr[t].astype(F32)).astype(BF16)
        for c_ in range(2):
            out[(c_ + c) % 2, pl.ds(t * rows, rows), :] = value[c_]

    for t in range(CHUNKS):
        gather_1(t)
    for t in range(CHUNKS):
        gather_2(t)
        gather_3(t)
    gather_4(0)
    gather_5(0)
    loads["d2"].wait()
    dot_2(0)
    gather_4(1)
    loads["d1"].wait()
    dot_1(0)
    gather_5(1)
    sum2_1(0)
    dot_2(1)
    sum1_1(0)
    sum2_2(0)
    dot_1(1)
    sum1_2(0)
    sum2_3(0)
    sum2_1(1)
    sum1_1(1)
    sum1_3(0)
    loads["gv"].wait()
    loads["uv"].wait()
    sum2_4(0)
    all2_1(0)
    sum2_2(1)
    sum1_2(1)
    sum1_4(0)
    all1_1(0)
    sum2_3(1)
    sum1_3(1)
    all2_2(0)
    all1_2(0)
    sum2_4(1)
    all2_1(1)
    sum1_4(1)
    all1_1(1)
    all2_3(0)
    all1_3(0)
    all2_2(1)
    all1_2(1)
    all1_4(0)
    all2_4(0)
    all2_3(1)
    all1_3(1)
    all1_5(0)
    loads["wg"].wait()
    loads["wu"].wait()
    dot_3(0)
    all1_4(1)
    all2_5(0)
    dot_4(0)
    all2_4(1)
    down_1(0)
    all1_5(1)
    dot_3(1)
    down_2(0)
    all2_5(1)
    down_3(0)
    dot_4(1)
    down_1(1)
    down_4(0)
    down_2(1)
    down_3(1)
    down_4(1)
    net.finish()


def solution(mesh):
    assert mesh.shape["row"] == 16 and mesh.shape["col"] == 8

    def per_device(out_grad, gate_saved, up_saved, gate_weight, up_weight, down_weight):
        hidden = gate_saved.shape[1]
        depth = out_grad.shape[1]
        tiles = hidden // LANES
        wide1 = (tiles + 1) // 2 * LANES
        wide2 = hidden - wide1
        rows = gate_saved.shape[0] // CHUNKS
        n = CHUNKS
        scratch = [
            pltpu.VMEM((n, 2, 8, rows, depth), BF16),
            pltpu.VMEM(down_weight.shape, BF16),
            pltpu.VMEM(gate_weight.shape, BF16),
            pltpu.VMEM(up_weight.shape, BF16),
            pltpu.VMEM(gate_saved.shape, BF16),
            pltpu.VMEM(up_saved.shape, BF16),
            pltpu.VMEM((n, 8, rows, wide1), F32),
            pltpu.VMEM((n, 8, rows, wide2), F32),
            pltpu.VMEM((n, 8, rows, wide1), BF16),
            pltpu.VMEM((n, 8, rows, wide2), BF16),
            pltpu.VMEM((n, 8, rows, wide1), BF16),
            pltpu.VMEM((n, 8, rows, wide2), BF16),
            pltpu.VMEM((n, 2, 3, 2, rows, wide1 // 2), BF16),
            pltpu.VMEM((n, 2, 3, 2, rows, wide1 // 2), BF16),
            pltpu.VMEM((n, 2, 3, rows, wide2 // 2), BF16),
            pltpu.VMEM((n, 2, 3, rows, wide2 // 2), BF16),
            pltpu.VMEM((n, rows, wide1), BF16),
            pltpu.VMEM((n, rows, wide1), BF16),
            pltpu.VMEM((n, rows, wide1), F32),
            pltpu.VMEM((n, 4, rows, wide2), BF16),
            pltpu.VMEM((n, 4, rows, wide2), BF16),
            pltpu.VMEM((n, 2, 2, 8, rows, wide1), BF16),
            pltpu.VMEM((n, 2, 2, 8, rows, wide2), BF16),
            pltpu.VMEM((n, 2, 8, rows, depth), F32),
            pltpu.VMEM((n, 2, 3, 2, 2, rows, depth // 2), BF16),
            pltpu.VMEM((n, 2, 3, 2, 2, rows, depth // 2), BF16),
            pltpu.VMEM((n, 2, rows, depth), F32),
            pltpu.VMEM((n, 2, rows, depth), BF16),
            pltpu.VMEM((n, 2, rows, depth), BF16),
            pltpu.SemaphoreType.DMA((6 + 2 * n,)),
            pltpu.SemaphoreType.DMA((70 * n,)),
            pltpu.SemaphoreType.DMA((70 * n,)),
        ]
        result = pl.pallas_call(
            kernel,
            out_shape=jax.ShapeDtypeStruct((2, gate_saved.shape[0], depth), BF16),
            in_specs=[pl.BlockSpec(memory_space=pl.ANY)] * 6,
            out_specs=pl.BlockSpec(memory_space=pltpu.VMEM),
            scratch_shapes=scratch,
            compiler_params=pltpu.CompilerParams(
                collective_id=0,
                has_side_effects=True,
                vmem_limit_bytes=60 * 1024 * 1024,
            ),
        )(out_grad, gate_saved, up_saved, gate_weight, up_weight, down_weight)
        return result.reshape(out_grad.shape)

    placed = (
        P("col", "row"),
        P("row", "col"),
        P("row", "col"),
        P("row", "col"),
        P("row", "col"),
        P("col", "row"),
    )
    return jax.shard_map(
        per_device, mesh=mesh, in_specs=placed, out_specs=P("col", "row"), check_vma=False
    )
```

time: 247 us -> 92.3 us (0.37)
  waiting for transfers between devices: 147 us -> 0 us
  Pallas kernels: 0 us -> 90.6 us
  blocking collectives: 60.1 us -> 0 us
  matrix products: 22.5 us -> 0 us
  between operations: 13.1 us -> 0.01 us
  other arithmetic: 2.77 us -> 0 us
    pallas_call x0 -> x1, Pallas kernels: none -> 90.6 us  [per_device(): pl.pallas_call(kernel, out_shape=jax.ShapeDtypeStruct((2, gate_saved.shap...]
    reduce_scatter x1 -> x0, waiting for transfers between devices: 79 us -> none  [per_device(): lax.psum_scatter(partial_hidden, 'row', scatter_dimension=0, tiled=True)]
    all_gather x2 -> x0, waiting for transfers between devices: 66.9 us -> none  [per_device(): block_pair = lax.all_gather((gate_grad, up_grad), 'row', axis=0, tiled=True)]
    all_to_all x2 -> x0, blocking collectives: 60.1 us -> none  [the longest x1 35.2 us: sent_and_summed(): lax.all_to_all(blocks, axis, split_axis=0, concat_axis=0, tiled=True)]
    dot_general x3 -> x0, matrix products: 22.5 us -> none  [contract_last(): lax.dot_general(left, right, (((1,), (1,)), ((), ())), preferred_element_...]
  transfers between devices with their start and end apart: 3 -> 0, of which waited for: 3 -> 0; matrix products, arithmetic and copies ran while one was open for 3% -> 0% of each run, Pallas kernels for 0% -> 0%
where the time goes in v1:
time: 92.3 us; the launch traced here: 92.2 us
  Pallas kernels  90.6 us (98%)
  local copies, waits for them, and re-layouts  1.57 us (2%)
    pallas_call x1, Pallas kernels, per_device(): pl.pallas_call(kernel, out_shape=jax.ShapeDtypeStruct((2, gate_saved.shap...  90.6 us

profile of v1, /device:TPU:0, one launch (start us, length us, event | category | flops | bytes accessed | tf_op | source)
XLA Modules:
  0.0 92.2 jit_solution(8413003713318495597)
XLA Ops:
  0.0 90.6 %shard_map.64 = bf16[2,32,1024]{2,1,0:T(8,128)(2,1)} custom-call(bf16[64,1024]{1,0:T(8,128)(2,1)} %og.1, bf16[32,3328]{1,0:T(8,128)(2,1)} %gs.1, bf16[32,3328]{1,0:T(8,128)(2,1)} %us.1, bf16[1024,3328]{1,0:T(8,128)(2,1)} %gw.1, bf16[1024,3328]{1,0:T(8,128)(2,1)} %uw.1, bf16[3328,1024]{1,0:T(8,128)(2,1)} %dw.1), custom_call_target="tpu_custom_call" | custom-call | tf_op jit(solution)/shard_map/pallas_call | solution.py:502
  90.6 1.6 %copy.8 = bf16[64,1024]{1,0:T(8,128)(2,1)} copy(bf16[64,1024]{1,0:T(8,128)(2,1)} %bitcast.1) | data formatting | bytes 262144
